TPU v7x, 512 devices: a whole 4x8x8 slice. The times are simulated.
512 devices in a mesh: basis: 32 (over x, z), angle: 8 (over y), pol: 2 (over core).
Axes of the slice: x: 4, y: 8, z: 8, core: 2. Of those that a mesh axis runs over, the one named last changes fastest.
Arguments:
- adjoint: float32 [2, 128, 256, 2, 128], P('pol', 'angle', 'basis'), may hold values from -6 to 6
- currents: float32 [2, 128, 256, 2, 128], P('pol', 'angle', 'basis'), may hold values from -6 to 6
- radiation: float32 [2, 128, 256, 2, 128], P('pol', 'angle', 'basis'), may hold values from -6 to 6
- near_blocks: bfloat16 [256, 6, 2, 128, 128], P('basis'), may hold values from -0.15625 to 0.15625
- inverse_blocks: bfloat16 [256, 2, 128, 128], P('basis'), may hold values from -0.375 to 0.375
- col_device: int32 [256, 6], P('basis'), may hold values from 0 to 31, all different within a row; in each aligned block of 8 rows (0 to 7, 8 to 15, ...) at most 3 rows name the same one
- col_offset: int32 [256, 6], P('basis'), may hold values from 0 to 7
- box_of_block: int32 [256], P('basis'), may hold values from 0 to 127
- pair_rate: float32 [256, 6], P('basis'), may hold values from -4 to 4
Outputs:
- updated: float32 [2, 128, 256, 2, 128], P('pol', 'angle', 'basis')
- shape_grad: float32 [128], P('basis')
Inputs may be any that keep to these rules, and one draw needn't show every extreme that they name: `col_device`: each row names 6 different devices; the rows of one basis device name any device at most 3 times, and in some devices' rows one device exactly 3 times.
All inputs are finite; a program needn't handle non-finite values.
Results may differ from a plain program's by a relative error of at most 0.0033.
Values sent between devices are 32-bit elements; how exact they have to be, the bound alone decides.
A program may use at most 64 MiB of HBM per device.

v0:
```python
import math

import jax
import jax.numpy as jnp
from jax import lax
from jax.sharding import PartitionSpec as P

BOX_DEV = 4


def conjugate_pairs(matrices, vectors):
    products = jnp.einsum(
        "rjcnm,radn->rjcdam", matrices, vectors, preferred_element_type=jnp.float32
    )
    real_part = products[:, :, 0, 0] + products[:, :, 1, 1]
    imag_part = products[:, :, 0, 1] - products[:, :, 1, 0]
    return jnp.stack([real_part, imag_part], axis=3)


def on_device(
    adjoint,
    currents,
    radiation,
    near_blocks,
    inverse_blocks,
    col_device,
    col_offset,
    box_of_block,
    pair_rate,
):
    highest = lax.Precision.HIGHEST
    angles_here = adjoint.shape[1]
    blocks = adjoint.shape[2]
    unknowns = adjoint.shape[4]
    near_count = near_blocks.shape[1]
    pairs = blocks * near_count
    record = angles_here * 2 * unknowns
    basis_count = lax.axis_size("basis")
    angles_all = angles_here * lax.axis_size("angle")
    rad_real = radiation[0, :, :, 0, :]
    rad_imag = radiation[0, :, :, 1, :]
    cur_real = currents[0, :, :, 0, :]
    cur_imag = currents[0, :, :, 1, :]
    part_real = jnp.sum(rad_real * cur_real - rad_imag * cur_imag, axis=(1, 2))
    part_imag = jnp.sum(rad_real * cur_imag + rad_imag * cur_real, axis=(1, 2))
    far_real, far_imag = lax.psum((part_real, part_imag), "basis")
    norm_far = 1.0 / math.sqrt(blocks * basis_count * unknowns)
    far_real = (far_real * norm_far)[:, None, None]
    far_imag = (far_imag * norm_far)[:, None, None]
    source = jnp.stack(
        [far_real * rad_real + far_imag * rad_imag, far_imag * rad_real - far_real * rad_imag],
        axis=2,
    )
    rounded = adjoint[0].astype(jnp.bfloat16)
    vectors = jnp.transpose(rounded, (1, 0, 2, 3))
    terms = conjugate_pairs(near_blocks, vectors)
    flat_terms = terms.reshape(pairs, record)
    target = col_device.reshape(pairs)
    offset_flat = col_offset.reshape(pairs)
    rate_flat = pair_rate.reshape(pairs)
    box_pairs = jnp.repeat(box_of_block, near_count)
    cur_rows = jnp.transpose(currents[0], (1, 0, 2, 3)).reshape(blocks, record)
    box_range = lax.iota(jnp.int32, BOX_DEV * basis_count)
    global_col = target * blocks + offset_flat
    rows_here = lax.iota(jnp.int32, blocks * lax.axis_size("basis"))
    chosen = (rows_here[:, None] == global_col[None, :]).astype(jnp.float32)
    received = lax.psum_scatter(
        jnp.dot(chosen, flat_terms, precision=highest, preferred_element_type=jnp.float32),
        "basis",
        scatter_dimension=0,
        tiled=True,
    )
    every_row = lax.all_gather(cur_rows, "basis", axis=0, tiled=True)
    beside = jnp.take(every_row, global_col, axis=0)
    values = rate_flat * jnp.sum(flat_terms * beside, axis=1)
    box_table = (box_pairs[:, None] == box_range[None, :]).astype(jnp.float32)
    partial_grad = jnp.dot(values, box_table, precision=highest, preferred_element_type=jnp.float32)
    total_grad = lax.psum(partial_grad, ("basis", "angle", "pol"))
    share = lax.dynamic_slice_in_dim(total_grad, lax.axis_index("basis") * BOX_DEV, BOX_DEV)
    shape_grad = share * (-1.0 / math.sqrt(4 * unknowns * angles_all * near_count))
    column_sums = jnp.transpose(received.reshape(blocks, angles_here, 2, unknowns), (1, 0, 2, 3))
    residual = (source - column_sums).astype(jnp.bfloat16)
    res_rows = jnp.transpose(residual, (1, 0, 2, 3))
    update = conjugate_pairs(inverse_blocks[:, None], res_rows)[:, 0]
    updated = adjoint[0] + jnp.transpose(update, (1, 0, 2, 3))
    return (updated[None], shape_grad)


def solution(mesh):
    placed = (
        P("pol", "angle", "basis", None, None),
        P("pol", "angle", "basis", None, None),
        P("pol", "angle", "basis", None, None),
        P("basis", None, None, None, None),
        P("basis", None, None, None),
        P("basis", None),
        P("basis", None),
        P("basis"),
        P("basis", None),
    )
    return jax.shard_map(
        on_device,
        mesh=mesh,
        in_specs=placed,
        out_specs=(P("pol", "angle", "basis", None, None), P("basis")),
        check_vma=False,
    )
```

profile of v0, /device:TPU:1, one launch (start us, length us, event | category | flops | bytes accessed | tf_op | source)
XLA Modules:
  0.0 338.8 jit_solution(205261647979174648)
XLA Ops:
  7.2 0.0 copy-start
  7.2 0.0 all-gather.2.cloned.1.call-start
  7.2 1.7 copy.40
  8.9 0.0 all-gather.2.cloned.1.call-update
  9.0 0.0 reduce-scatter.2.cloned.1.call-start
  9.0 0.7 compare_and_fusion
  9.7 0.1 add.104
  9.8 0.0 copy-done
  9.8 1.4 fusion.2
  11.3 0.1 fusion.6
  11.4 0.1 pad_maximum_fusion
  11.4 1.5 copy.35
  12.9 2.7 reshape.232
  15.6 4.9 %fusion.12 = f32[256,4096]{1,0:T(8,128)} fusion(f32[48,4096]{1,0:T(8,128)} %reshape.232, s32[48]{0:T(128)S(1)} %add.104), kind=kOutput, calls=%fused_computation.22 | convolution fusion | flops 603992064 | bytes 4980928 | tf_op jit(solution)/shard_map/dot_general | solution.py:68
  20.5 0.0 copy-start.1
  20.5 0.0 copy-start.3
  20.5 0.0 copy-start.4
  20.5 0.0 copy-start.5
  20.5 0.0 reduce-scatter.2.cloned.1.call-update
  20.6 0.9 copy-done.1
  21.4 0.1 fusion.23
  21.5 0.0 copy-done.3
  21.5 0.1 fusion.24
  21.7 0.2 subtract_reduce_fusion
  21.9 68.3 %all-reduce = (f32[16]{0:T(128)S(1)}, f32[16]{0:T(128)S(1)}) all-reduce(f32[16]{0:T(128)S(1)} %get-tuple-element.7, f32[16]{0:T(128)S(1)} %get-tuple-element.6), channel_id=1, replica_groups=mesh['basis'=32,'angle'=8,'pol'=2] {'basis'}, use_global_device_ids=true, to_apply=%region_3.0 | all-reduce | flops 32 | bytes 256 | tf_op jit(solution)/shard_map/psum | solution.py:46
  90.1 0.1 add.112
  90.2 0.0 copy-done.4
  90.2 0.1 reshape.234
  90.3 0.0 copy-done.5
  90.3 0.1 broadcast_in_dim.28
  90.4 0.1 eq.31
  90.4 0.1 broadcast_in_dim.25
  90.6 0.1 multiply_add_fusion
  90.7 11.7 %all-gather.2.cloned.1.call-done = f32[256,4096]{1,0:T(8,128)} async-done(((f32[8,4096]{1,0:T(8,128)}), f32[256,4096]{1,0:T(8,128)}) %all-gather.2.cloned.1.call-update) | async-done | bytes 4194320 | tf_op jit(solution)/shard_map/all_gather | solution.py:73
  102.4 4.2 %gather_fusion = f32[48,4096]{1,0:T(8,128)} fusion(f32[256,4096]{1,0:T(8,128)} %all-gather.2.cloned.1.call-done, s32[1024]{0:T(1024)S(1)} %pad_clamp_fusion), kind=kCustom, calls=%fused_computation | custom fusion | bytes 1573056 | tf_op jit(solution)/shard_map/jit(_take)/gather | solution.py:74
  106.6 0.0 copy-start.2
  106.6 1.7 multiply_reduce_fusion
  108.2 0.2 convolution_bitcast_fusion.1
  108.4 100.0 %psum.23 = f32[128]{0:T(128)S(1)} all-reduce(f32[128]{0:T(128)S(1)} %convolution_bitcast_fusion.1), channel_id=1, replica_groups=mesh['basis'=32,'angle'=8,'pol'=2] {'basis','angle','pol'}, use_global_device_ids=true, to_apply=%region_6.7 | all-reduce | flops 128 | bytes 1024 | tf_op jit(solution)/shard_map/psum | solution.py:78
  208.4 0.6 dynamic-slice_multiply_fusion
  209.0 119.9 %reduce-scatter.2.cloned.1.call-done = f32[8,4096]{1,0:T(8,128)} async-done(((f32[256,4096]{1,0:T(8,128)}), f32[8,4096]{1,0:T(8,128)}) %reduce-scatter.2.cloned.1.call-update) | async-done | bytes 131088 | tf_op jit(solution)/shard_map/reduce_scatter | solution.py:67
  329.0 0.9 fusion.14
  329.9 1.2 convolution_bitcast_fusion
  331.2 0.0 copy-done.2
  331.2 0.1 fusion.11
  331.2 0.8 copy.41
  (6 shorter events, 0.1 us)
Async XLA Ops:
  7.2 2.7 copy-start
  7.2 95.2 %all-gather.2.cloned.1.call-start = ((), (), s32[]{:S(2)}) async-start(), calls=%async_computation.2 | async-start | bytes 4325376 | tf_op jit(solution)/shard_map/all_gather | solution.py:73
  9.0 320.0 %reduce-scatter.2.cloned.1.call-start = ((), (), s32[]{:S(2)}) async-start(), calls=%async_computation.1 | async-start | bytes 4325376 | tf_op jit(solution)/shard_map/reduce_scatter | solution.py:67
  20.5 0.9 copy-start.1
  20.5 1.0 copy-start.3
  20.5 69.7 %copy-start.4 = (f32[8,6]{1,0:T(8,128)S(1)}, f32[8,6]{1,0:T(8,128)}, u32[]{:S(2)}) copy-start(f32[8,6]{1,0:T(8,128)} %param.17) | copy-start | bytes 580
  20.5 69.8 %copy-start.5 = (s32[8]{0:T(128)S(1)}, s32[8]{0:T(128)}, u32[]{:S(2)}) copy-start(s32[8]{0:T(128)} %param.16) | copy-start | bytes 100
  106.6 224.6 %copy-start.2 = (f32[1,16,8,2,128]{4,3,2,1,0:T(2,128)S(1)}, f32[1,16,8,2,128]{4,3,2,1,0:T(2,128)}, u32[]{:S(2)}) copy-start(f32[1,16,8,2,128]{4,3,2,1,0:T(2,128)} %param.9) | copy-start | bytes 393220
Sparse Core Ops, SparseCore 0:
  11.8 90.5 all-gather.1
  106.8 222.0 reduce-scatter.1
where the time goes:
time: 343 us; the launch traced here: 339 us
  blocking collectives  168 us (49%)
  waiting for transfers between devices  132 us (38%)
  between operations  14.2 us (4%)
  local copies, waits for them, and re-layouts  12.4 us (4%)
  matrix products  7.77 us (2%)
  other arithmetic  4.44 us (1%)
    reduce_scatter x1, waiting for transfers between devices, on_device(): lax.psum_scatter(jnp.dot(chosen, flat_terms, precision=highest, preferred...  120 us
    psum x1, blocking collectives, on_device(): total_grad = lax.psum(partial_grad, ('basis', 'angle', 'pol'))  100 us
    psum x1, blocking collectives, on_device(): far_real, far_imag = lax.psum((part_real, part_imag), 'basis')  68.3 us
    all_gather x1, waiting for transfers between devices, on_device(): every_row = lax.all_gather(cur_rows, 'basis', axis=0, tiled=True)  11.7 us
  transfers between devices with their start and end apart: 2, of which 2 were waited for; matrix products, arithmetic and copies ran while one was open for 6% of the time, Pallas kernels for 0%

commit v1 on v0

v1 whole, which is shorter than its diff:
```python
import functools
import math

import jax
import jax.numpy as jnp
from jax import lax
from jax.experimental import pallas as pl
from jax.experimental.pallas import tpu as pltpu
from jax.sharding import PartitionSpec as P

MESH = pl.DeviceIdType.MESH
F32 = jnp.float32
BF16 = jnp.bfloat16

NX, NZ = 4, 8
CAP = 3
BOX_DEV = 4
ORDER = (4, 3, 5, 2, 6, 1, 7, 0)
PLACE = {distance % NZ: place for place, distance in enumerate(ORDER)}


def kernel(
    sizes,
    pair_tab,
    adj,
    cur,
    rad,
    off_tab,
    rate_box_tab,
    near_hbm,
    inv_hbm,
    out,
    grad,
    near,
    inv,
    lhs,
    sent,
    got,
    cur_at,
    part,
    part_got,
    own_sum,
    msg,
    msg_got,
    far_sum,
    far_got,
    lane_dots,
    g_sum,
    g_got,
    local_sem,
    term_s,
    term_r,
    cur_s,
    cur_r,
    part_s,
    part_r,
    msg_s,
    msg_r,
    far_s,
    far_r,
    g_s,
    g_r,
):
    ny, nc, norm_far = sizes
    blocks = 8
    b = lax.axis_index("basis")
    y = lax.axis_index("angle")
    c0 = lax.axis_index("pol")
    x = lax.div(b, NZ)
    z = lax.rem(b, NZ)

    def at(dx=0, dz=0, dy=0, dc=0):
        basis = lax.rem(x + dx, NX) * NZ + lax.rem(z + dz, NZ)
        return (basis, lax.rem(y + dy, ny), lax.rem(c0 + dc, nc))

    def remote(src, dst, send_sem, recv_sem, device):
        return pltpu.make_async_remote_copy(
            src_ref=src,
            dst_ref=dst,
            send_sem=send_sem,
            recv_sem=recv_sem,
            device_id=device,
            device_id_type=MESH,
        )

    near_copy = pltpu.make_async_copy(near_hbm, near, local_sem.at[0])
    inv_copy = pltpu.make_async_copy(inv_hbm, inv, local_sem.at[1])
    near_copy.start()
    inv_copy.start()

    xc = [(dx, dc) for dx in range(NX) for dc in range(nc) if dx or dc]
    groups = [
        [(dx * nc + dc, at(dx=dx, dc=dc)) for dx, dc in xc],
        [(dz, at(dz=dz)) for dz in range(1, NZ)],
        [(dy, at(dy=dy)) for dy in range(1, ny)],
    ]
    barrier = pltpu.get_barrier_semaphore()
    for group in groups:
        for _, device in group:
            pl.semaphore_signal(barrier, inc=1, device_id=device, device_id_type=MESH)

    far_re = jnp.zeros((16, 128), F32)
    far_im = jnp.zeros((16, 128), F32)
    for r in range(blocks):
        re = pl.ds(2 * r, 16, stride=16)
        im = pl.ds(2 * r + 1, 16, stride=16)
        ar, ai = adj[re, :].astype(BF16), adj[im, :].astype(BF16)
        lhs[r, 0:16, 0:128] = ar
        lhs[r, 0:16, 128:256] = ai
        lhs[r, 16:32, 0:128] = ai
        lhs[r, 16:32, 128:256] = -ar
        cr, ci = cur[re, :], cur[im, :]
        cur_at[PLACE[0], r, 0:2] = cr.reshape(2, 8, 128)
        cur_at[PLACE[0], r, 2:4] = ci.reshape(2, 8, 128)
        rr, ri = rad[re, :], rad[im, :]
        far_re += rr * cr - ri * ci
        far_im += rr * ci + ri * cr
    lane = lax.broadcasted_iota(jnp.int32, (16, 128), 1)
    far_tile = jnp.where(
        lane < 64,
        jnp.sum(far_re, axis=1, keepdims=True),
        jnp.sum(far_im, axis=1, keepdims=True),
    )
    for k in range(NX):
        msg[k, 0:16] = far_tile
        msg[k, 16:40] = off_tab[k]
        msg[k, 40:64] = rate_box_tab[k]
    msg_got[0] = msg[0]

    pl.semaphore_wait(barrier, sum(len(group) for group in groups))

    msgs = [
        remote(msg.at[k], msg_got.at[k], msg_s.at[k], msg_r.at[k], at(dx=k))
        for k in range(1, NX)
    ]
    for copy in msgs:
        copy.start()

    half = blocks // 2

    def cur_step(way, step):
        sign = 1 if way == 0 else -1
        have = PLACE[(-sign * (step - 1)) % NZ]
        want = PLACE[(-sign * step) % NZ]
        rows = slice(None) if step < 4 else slice(way * half, (way + 1) * half)
        return remote(
            cur_at.at[have, rows],
            cur_at.at[want, rows],
            cur_s.at[way, step - 1],
            cur_r.at[way, step - 1],
            at(dz=sign % NZ),
        )

    cur_copies = {(way, step): cur_step(way, step) for way in (0, 1) for step in range(1, 5)}

    def forward_currents(step):
        for way in (0, 1):
            cur_copies[way, step - 1].wait_recv()
            cur_copies[way, step].start()

    for way in (0, 1):
        cur_copies[way, 1].start()
    near_copy.wait()

    def term_copy(place, k):
        return remote(
            sent.at[place, k - 1],
            got.at[place, k],
            term_s.at[place, k - 1],
            term_r.at[place, k - 1],
            at(dx=k),
        )

    def send_terms(place, _):
        for k in (2, 1, 3, 0):
            for s in range(CAP):
                pair = pair_tab[k * NZ * CAP + place * CAP + s]
                term = jnp.dot(
                    lhs[lax.div(pair, 6)], near[pair], preferred_element_type=F32
                ).reshape(4, 8, 128)
                if k:
                    sent[place, k - 1, s] = term
                else:
                    got[place, 0, s] = term
            if k:
                term_copy(place, k).start()
        return 0

    lax.fori_loop(0, 2, send_terms, 0)

    for copy in msgs:
        copy.wait_recv()
    far_sum[...] = msg_got[0, 0:16] + msg_got[1, 0:16] + msg_got[2, 0:16] + msg_got[3, 0:16]
    fars = [
        remote(far_sum, far_got.at[k], far_s.at[k], far_r.at[k], at(dz=k)) for k in range(1, NZ)
    ]
    for copy in fars:
        copy.start()

    lax.fori_loop(2, 4, send_terms, 0)
    forward_currents(2)
    lax.fori_loop(4, 6, send_terms, 0)
    forward_currents(3)
    lax.fori_loop(6, 8, send_terms, 0)
    forward_currents(4)

    def masks(place, k, s):
        row = 16 + place * CAP + s
        off = jnp.broadcast_to(msg_got[k, row : row + 1, :], (8, 128))
        return [(off == float(c))[None] for c in range(blocks)]

    def combine(place):
        for k in range(1, NX):
            term_copy(place, k).wait_recv()
        sums = [jnp.zeros((4, 8, 128), F32) for _ in range(blocks)]
        for k in range(NX):
            for s in range(CAP):
                term = got[place, k, s]
                for c, mask in enumerate(masks(place, k, s)):
                    sums[c] = sums[c] + jnp.where(mask, term, 0.0)
        return sums

    def dots(place):
        for k in range(NX):
            for s in range(CAP):
                chosen = jnp.zeros((4, 8, 128), F32)
                for c, mask in enumerate(masks(place, k, s)):
                    chosen = jnp.where(mask, cur_at[place, c], chosen)
                product = jnp.sum(got[place, k, s] * chosen, axis=0)
                lane_dots[k, place * CAP + s : place * CAP + s + 1, :] = jnp.sum(
                    product, axis=0, keepdims=True
                )

    def part_copy(way, hops):
        rows = slice(None) if hops < 4 else slice(way * half, (way + 1) * half)
        return remote(
            part.at[way, hops - 1, rows],
            part_got.at[way, hops - 1, rows],
            part_s.at[way, hops - 1],
            part_r.at[way, hops - 1],
            at(dz=1 if way == 0 else NZ - 1),
        )

    part_copies = {(way, hops): part_copy(way, hops) for way in (0, 1) for hops in range(1, 5)}

    sums = combine(PLACE[4])
    for way in (0, 1):
        for c in range(way * half, (way + 1) * half):
            part[way, 3, c] = sums[c]
        part_copies[way, 4].start()
    for hops in (3, 2, 1):
        for way in (0, 1):
            sums = combine(PLACE[hops if way == 0 else NZ - hops])
            part_copies[way, hops + 1].wait_recv()
            for c in range(blocks):
                if hops < 3 or way * half <= c < (way + 1) * half:
                    sums[c] = sums[c] + part_got[way, hops, c]
                part[way, hops - 1, c] = sums[c]
            part_copies[way, hops].start()
    sums = combine(PLACE[0])
    for c in range(blocks):
        own_sum[c] = sums[c]

    for place in (7, 5, 6, 3, 4, 1, 2):
        dots(place)
    for way in (0, 1):
        cur_copies[way, 4].wait_recv()
    dots(0)

    value = jnp.zeros((8, 128), F32)
    box_lane = lax.broadcasted_iota(jnp.int32, (NZ * CAP, 128), 1).astype(F32)
    for k in range(NX):
        rate = msg_got[k, 40:64, 0:1]
        box = msg_got[k, 40:64, 64:65]
        pair_value = rate * jnp.sum(lane_dots[k], axis=1, keepdims=True)
        table = jnp.where(box_lane == box, pair_value, 0.0)
        value += table[0:8] + table[8:16] + table[16:24]
    g_sum[0] = value

    def g_copies(stage):
        return [
            remote(
                g_sum.at[stage],
                g_got.at[stage, place],
                g_s.at[stage, place],
                g_r.at[stage, place],
                device,
            )
            for place, device in groups[stage]
        ]

    g_all = [g_copies(stage) for stage in range(3)]

    def g_gather(stage):
        total = g_sum[stage]
        for (place, _), copy in zip(groups[stage], g_all[stage]):
            copy.wait_recv()
            total = total + g_got[stage, place]
        return total

    for copy in g_all[0]:
        copy.start()

    for copy in fars:
        copy.wait_recv()
    far = far_sum[...]
    for k in range(1, NZ):
        far = far + far_got[k]
    far = far * norm_far
    far_re = jnp.broadcast_to(far[:, 0:1], (16, 128))
    far_im = jnp.broadcast_to(far[:, 64:65], (16, 128))

    g_sum[1] = g_gather(0)
    for copy in g_all[1]:
        copy.start()

    inv_copy.wait()
    for way in (0, 1):
        part_copies[way, 1].wait_recv()
    for c in range(blocks):
        re = pl.ds(2 * c, 16, stride=16)
        im = pl.ds(2 * c + 1, 16, stride=16)
        rr, ri = rad[re, :], rad[im, :]
        total = (own_sum[c] + (part_got[0, 0, c] + part_got[1, 0, c])).reshape(32, 128)
        res_re = ((far_re * rr + far_im * ri) - total[0:16]).astype(BF16)
        res_im = ((far_im * rr - far_re * ri) - total[16:32]).astype(BF16)
        lhs[c, 0:16, 0:128] = res_re
        lhs[c, 0:16, 128:256] = res_im
        lhs[c, 16:32, 0:128] = res_im
        lhs[c, 16:32, 128:256] = -res_re
        update = jnp.dot(lhs[c], inv[c], preferred_element_type=F32)
        out[re, :] = adj[re, :] + update[0:16]
        out[im, :] = adj[im, :] + update[16:32]

    g_sum[2] = g_gather(1)
    for copy in g_all[2]:
        copy.start()
    total = jnp.sum(g_gather(2), axis=0, keepdims=True)
    grad[...] = jnp.broadcast_to(total, (8, 128))

    for copy in msgs + fars + g_all[0] + g_all[1] + g_all[2]:
        copy.wait_send()
    for way in (0, 1):
        for step in range(1, 5):
            cur_copies[way, step].wait_send()
            part_copies[way, step].wait_send()

    def terms_gone(place, _):
        for k in range(1, NX):
            term_copy(place, k).wait_send()
        return 0

    lax.fori_loop(0, NZ, terms_gone, 0)


def on_device(
    adjoint,
    currents,
    radiation,
    near_blocks,
    inverse_blocks,
    col_device,
    col_offset,
    box_of_block,
    pair_rate,
):
    angles_here, blocks, unknowns = adjoint.shape[1], adjoint.shape[2], adjoint.shape[4]
    near_count = near_blocks.shape[1]
    pairs = blocks * near_count
    ny, nc = lax.axis_size("angle"), lax.axis_size("pol")
    basis_count = lax.axis_size("basis")
    rows = angles_here * blocks * 2

    me = lax.axis_index("basis")
    target = col_device.reshape(pairs)
    far_x = (target // NZ - me // NZ) % NX
    far_z = (target % NZ - me % NZ) % NZ
    place = sum(jnp.where(far_z == d, i, 0) for i, d in enumerate(ORDER))
    number = lax.iota(jnp.int32, pairs)
    rank = jnp.sum(
        (target[:, None] == target[None, :]) & (number[None, :] < number[:, None]),
        axis=1,
        dtype=jnp.int32,
    )
    slot = (far_x * NZ + place) * CAP + rank
    slots = NX * NZ * CAP
    hot = slot[None, :] == lax.iota(jnp.int32, slots)[:, None]
    pair_tab = jnp.sum(jnp.where(hot, number[None, :], 0), axis=1)
    off = jnp.sum(jnp.where(hot, col_offset.reshape(1, pairs) + 1, 0), axis=1) - 1
    rate = jnp.sum(jnp.where(hot, pair_rate.reshape(1, pairs), 0.0), axis=1)
    box_pairs = jnp.repeat(box_of_block, near_count)
    box = jnp.sum(jnp.where(hot, box_pairs[None, :], 0), axis=1).astype(F32)
    lanes = lax.iota(jnp.int32, 128)[None, :]
    off_tab = jnp.broadcast_to(off.astype(F32)[:, None], (slots, 128)).reshape(NX, NZ * CAP, 128)
    rate_box = jnp.where(lanes < 64, rate[:, None], box[:, None]).reshape(NX, NZ * CAP, 128)

    vmem = pl.BlockSpec(memory_space=pltpu.VMEM)
    anywhere = pl.BlockSpec(memory_space=pl.ANY)
    dma = pltpu.SemaphoreType.DMA
    sizes = (ny, nc, 1.0 / math.sqrt(blocks * basis_count * unknowns))
    out, grad = pl.pallas_call(
        functools.partial(kernel, sizes),
        out_shape=(
            jax.ShapeDtypeStruct((rows, unknowns), F32),
            jax.ShapeDtypeStruct((8, 128), F32),
        ),
        in_specs=[pl.BlockSpec(memory_space=pltpu.SMEM)] + [vmem] * 5 + [anywhere] * 2,
        out_specs=(vmem, vmem),
        scratch_shapes=[
            pltpu.VMEM((pairs, 2 * unknowns, unknowns), BF16),
            pltpu.VMEM((blocks, 2 * unknowns, unknowns), BF16),
            pltpu.VMEM((blocks, 32, 256), BF16),
            pltpu.VMEM((NZ, NX - 1, CAP, 4, 8, 128), F32),
            pltpu.VMEM((NZ, NX, CAP, 4, 8, 128), F32),
            pltpu.VMEM((NZ, blocks, 4, 8, 128), F32),
            pltpu.VMEM((2, 4, blocks, 4, 8, 128), F32),
            pltpu.VMEM((2, 4, blocks, 4, 8, 128), F32),
            pltpu.VMEM((blocks, 4, 8, 128), F32),
            pltpu.VMEM((NX, 64, 128), F32),
            pltpu.VMEM((NX, 64, 128), F32),
            pltpu.VMEM((16, 128), F32),
            pltpu.VMEM((NZ, 16, 128), F32),
            pltpu.VMEM((NX, NZ * CAP, 128), F32),
            pltpu.VMEM((3, 8, 128), F32),
            pltpu.VMEM((3, 8, 8, 128), F32),
            dma((2,)),
            dma((NZ, NX - 1)),
            dma((NZ, NX - 1)),
            dma((2, 4)),
            dma((2, 4)),
            dma((2, 4)),
            dma((2, 4)),
            dma((NX,)),
            dma((NX,)),
            dma((NZ,)),
            dma((NZ,)),
            dma((3, 8)),
            dma((3, 8)),
        ],
        compiler_params=pltpu.CompilerParams(
            collective_id=0, has_side_effects=True, vmem_limit_bytes=40 << 20
        ),
        name="sweep",
    )(
        pair_tab,
        adjoint.reshape(rows, unknowns),
        currents.reshape(rows, unknowns),
        radiation.reshape(rows, unknowns),
        off_tab,
        rate_box,
        near_blocks.reshape(pairs, 2 * unknowns, unknowns),
        inverse_blocks.reshape(blocks, 2 * unknowns, unknowns),
    )
    share = lax.dynamic_slice_in_dim(grad[0], me * BOX_DEV, BOX_DEV)
    angles_all = angles_here * ny
    shape_grad = share * (-1.0 / math.sqrt(4 * unknowns * angles_all * near_count))
    return (out.reshape(adjoint.shape), shape_grad)


def solution(mesh):
    placed = (
        P("pol", "angle", "basis", None, None),
        P("pol", "angle", "basis", None, None),
        P("pol", "angle", "basis", None, None),
        P("basis", None, None, None, None),
        P("basis", None, None, None),
        P("basis", None),
        P("basis", None),
        P("basis"),
        P("basis", None),
    )
    return jax.shard_map(
        on_device,
        mesh=mesh,
        in_specs=placed,
        out_specs=(P("pol", "angle", "basis", None, None), P("basis")),
        check_vma=False,
    )
```

time: 343 us -> 72.2 us (0.21); the launches traced: 339 us -> 71.8 us
  blocking collectives: 168 us -> 0 us
  waiting for transfers between devices: 132 us -> 0 us
  Pallas kernels: 0 us -> 60.3 us
  between operations: 14.2 us -> 0.72 us
  matrix products: 7.77 us -> 0 us
    psum x2 -> x0, blocking collectives: 168 us -> none  [the longest x1 100 us: on_device(): total_grad = lax.psum(partial_grad, ('basis', 'angle', 'pol'))]
    reduce_scatter x1 -> x0, waiting for transfers between devices: 120 us -> none  [on_device(): lax.psum_scatter(jnp.dot(chosen, flat_terms, precision=highest, preferred...]
    pallas_call x0 -> x1, Pallas kernels: none -> 60.3 us  [on_device(): pl.pallas_call(functools.partial(kernel, sizes), out_shape=(jax.ShapeDtyp...]
    all_gather x1 -> x0, waiting for transfers between devices: 11.7 us -> none  [on_device(): every_row = lax.all_gather(cur_rows, 'basis', axis=0, tiled=True)]
    dot_general x4 -> x0, matrix products: 7.77 us -> none  [the longest x1 4.89 us: on_device(): jnp.dot(chosen, flat_terms, precision=highest, preferred_element_type=jnp...]
    unnamed x13 -> x11, local copies, waits for them, and re-layouts: 1.65 us -> 6.3 us
    gather x1 -> x0, local copies, waits for them, and re-layouts: 4.21 us -> none  [on_device(): beside = jnp.take(every_row, global_col, axis=0)]
  transfers between devices with their start and end apart: 2 -> 0, of which waited for: 2 -> 0; matrix products, arithmetic and copies ran while one was open for 6% -> 0% of each run, Pallas kernels for 0% -> 0%
where the time goes in v1:
time: 72.2 us; the launch traced here: 71.8 us
  Pallas kernels  60.3 us (84%)
  local copies, waits for them, and re-layouts  9.05 us (13%)
  other arithmetic  1.8 us (2%)
    pallas_call x1, Pallas kernels, on_device(): pl.pallas_call(functools.partial(kernel, sizes), out_shape=(jax.ShapeDtyp...  60.3 us
    unnamed x11, local copies, waits for them, and re-layouts  6.3 us

profile of v1, /device:TPU:1, one launch (start us, length us, event | category | flops | bytes accessed | tf_op | source)
XLA Modules:
  0.0 71.8 jit_solution(16473584838376822332)
XLA Ops:
  0.7 0.8 %reshape.182 = s32[48]{0:T(128)S(1)} reshape(s32[8,6]{1,0:T(8,128)} %param.14) | data formatting | bytes 384 | tf_op jit(solution)/shard_map/reshape | solution.py:375
  1.4 0.2 convert_reduce_fusion
  1.6 0.8 %broadcast_in_dim.109 = f32[48]{0:T(128)S(1)} reshape(f32[8,6]{1,0:T(8,128)} %param.17) | data formatting | bytes 384 | tf_op jit(solution)/shard_map/jit(_where)/broadcast_in_dim | solution.py:390
  2.4 0.1 select_reduce_fusion.1
  2.5 0.1 broadcast_in_dim.112
  2.6 0.7 broadcast_add_fusion
  3.3 0.1 add.127
  3.4 0.7 %broadcast_in_dim.114 = s32[8,6]{1,0:T(8,128)S(1)} broadcast(s32[8]{0:T(128)} %param.16), dimensions={0} | broadcast | bytes 224 | tf_op jit(solution)/shard_map/broadcast_in_dim | solution.py:391
  4.1 0.1 broadcast_in_dim.115
  4.2 0.1 select_reduce_fusion
  4.3 0.1 convert_element_type.25
  4.4 0.1 convert_element_type.27
  4.5 0.1 broadcast_select_fusion.rate_box_tab
  4.6 0.1 broadcast_in_dim.107.off_tab
  4.6 0.0 copy-start
  4.6 1.9 %copy-done = bf16[8,6,2,128,128]{4,3,2,1,0:T(8,128)(2,1)S(1)} copy-done((bf16[8,6,2,128,128]{4,3,2,1,0:T(8,128)(2,1)S(1)}, bf16[8,6,2,128,128]{4,3,2,1,0:T(8,128)(2,1)}, u32[]{:S(2)}) %copy-start) | copy-done | bytes 3145752
  6.5 0.0 copy-start.1
  6.5 1.0 %copy-done.1 = bf16[8,2,128,128]{3,2,1,0:T(8,128)(2,1)S(1)} copy-done((bf16[8,2,128,128]{3,2,1,0:T(8,128)(2,1)S(1)}, bf16[8,2,128,128]{3,2,1,0:T(8,128)(2,1)}, u32[]{:S(2)}) %copy-start.1) | copy-done | bytes 524312
  7.6 0.0 copy-start.2
  7.6 0.9 %copy-done.2 = f32[1,16,8,2,128]{4,3,2,1,0:T(2,128)S(1)} copy-done((f32[1,16,8,2,128]{4,3,2,1,0:T(2,128)S(1)}, f32[1,16,8,2,128]{4,3,2,1,0:T(2,128)}, u32[]{:S(2)}) %copy-start.2) | copy-done | bytes 131096
  8.5 0.0 copy-start.3
  8.5 0.9 %copy-done.3 = f32[1,16,8,2,128]{4,3,2,1,0:T(2,128)S(1)} copy-done((f32[1,16,8,2,128]{4,3,2,1,0:T(2,128)S(1)}, f32[1,16,8,2,128]{4,3,2,1,0:T(2,128)}, u32[]{:S(2)}) %copy-start.3) | copy-done | bytes 131096
  9.4 0.0 copy-start.4
  9.4 0.9 %copy-done.4 = f32[1,16,8,2,128]{4,3,2,1,0:T(2,128)S(1)} copy-done((f32[1,16,8,2,128]{4,3,2,1,0:T(2,128)S(1)}, f32[1,16,8,2,128]{4,3,2,1,0:T(2,128)}, u32[]{:S(2)}) %copy-start.4) | copy-done | bytes 131096
  10.3 60.3 %sweep.1 = (f32[256,128]{1,0:T(8,128)S(1)}, f32[8,128]{1,0:T(8,128)S(1)}) custom-call(s32[96]{0:T(128)S(1)} %get-tuple-element.8.pair_tab, f32[256,128]{1,0:T(8,128)S(1)} %bitcast.10, f32[256,128]{1,0:T(8,128)S(1)} %bitcast.11, f32[256,128]{1,0:T(8,128)S(1)} %bitcast.12, f32[4,24,128]{2,1,0:T(8,128)S(1)} %broadcast_in_dim.107.off_tab, ...), custom_call_target="tpu_custom_call" | custom-call | tf_op jit(solution)/shard_map/sweep/pallas_call | solution.py:401
  70.6 0.6 multiply_bitcast_fusion
  71.2 0.7 copy.12
  (5 shorter events, 0.0 us)
Async XLA Ops:
  4.6 1.9 %copy-start = (bf16[8,6,2,128,128]{4,3,2,1,0:T(8,128)(2,1)S(1)}, bf16[8,6,2,128,128]{4,3,2,1,0:T(8,128)(2,1)}, u32[]{:S(2)}) copy-start(bf16[8,6,2,128,128]{4,3,2,1,0:T(8,128)(2,1)} %param.12) | copy-start | bytes 9437188
  6.5 1.0 %copy-start.1 = (bf16[8,2,128,128]{3,2,1,0:T(8,128)(2,1)S(1)}, bf16[8,2,128,128]{3,2,1,0:T(8,128)(2,1)}, u32[]{:S(2)}) copy-start(bf16[8,2,128,128]{3,2,1,0:T(8,128)(2,1)} %param.13) | copy-start | bytes 1572868
  7.6 0.9 %copy-start.2 = (f32[1,16,8,2,128]{4,3,2,1,0:T(2,128)S(1)}, f32[1,16,8,2,128]{4,3,2,1,0:T(2,128)}, u32[]{:S(2)}) copy-start(f32[1,16,8,2,128]{4,3,2,1,0:T(2,128)} %param.9) | copy-start | bytes 393220
  8.5 0.9 %copy-start.3 = (f32[1,16,8,2,128]{4,3,2,1,0:T(2,128)S(1)}, f32[1,16,8,2,128]{4,3,2,1,0:T(2,128)}, u32[]{:S(2)}) copy-start(f32[1,16,8,2,128]{4,3,2,1,0:T(2,128)} %param.10) | copy-start | bytes 393220
  9.4 0.9 %copy-start.4 = (f32[1,16,8,2,128]{4,3,2,1,0:T(2,128)S(1)}, f32[1,16,8,2,128]{4,3,2,1,0:T(2,128)}, u32[]{:S(2)}) copy-start(f32[1,16,8,2,128]{4,3,2,1,0:T(2,128)} %param.11) | copy-start | bytes 393220

commit v2 on v1

v2 whole, which is shorter than its diff:
```python
import functools
import math

import jax
import jax.numpy as jnp
from jax import lax
from jax.experimental import pallas as pl
from jax.experimental.pallas import tpu as pltpu
from jax.sharding import PartitionSpec as P

MESH = pl.DeviceIdType.MESH
F32 = jnp.float32
BF16 = jnp.bfloat16

NX, NZ = 4, 8
CAP = 3
BOX_DEV = 4
ORDER = (4, 3, 5, 2, 6, 1, 7, 0)
PLACE = {distance % NZ: place for place, distance in enumerate(ORDER)}


def kernel(
    sizes,
    box_hbm,
    dev_hbm,
    off_hbm,
    rate_hbm,
    adj_hbm,
    cur_hbm,
    rad_hbm,
    near_hbm,
    inv_hbm,
    out,
    grad,
    box_of,
    dev,
    off_of,
    rate_of,
    adj,
    cur,
    rad,
    near,
    inv,
    tab_v,
    pair_tab,
    lhs,
    sent,
    got,
    cur_at,
    part,
    part_got,
    own_sum,
    msg,
    msg_got,
    far_sum,
    far_got,
    lane_dots,
    g_sum,
    g_got,
    local_sem,
    term_s,
    term_r,
    cur_s,
    cur_r,
    part_s,
    part_r,
    msg_s,
    msg_r,
    far_s,
    far_r,
    g_s,
    g_r,
):
    ny, nc, norm_far = sizes
    blocks, near_count = 8, 6
    pairs = blocks * near_count
    half = blocks // 2
    b = lax.axis_index("basis")
    y = lax.axis_index("angle")
    c0 = lax.axis_index("pol")
    x = lax.div(b, NZ)
    z = lax.rem(b, NZ)

    def at(dx=0, dz=0, dy=0, dc=0):
        basis = lax.rem(x + dx, NX) * NZ + lax.rem(z + dz, NZ)
        return (basis, lax.rem(y + dy, ny), lax.rem(c0 + dc, nc))

    def remote(src, dst, send_sem, recv_sem, device):
        return pltpu.make_async_remote_copy(
            src_ref=src,
            dst_ref=dst,
            send_sem=send_sem,
            recv_sem=recv_sem,
            device_id=device,
            device_id_type=MESH,
        )

    loads = [
        pltpu.make_async_copy(src, dst, local_sem.at[i])
        for i, (src, dst) in enumerate(
            [
                (box_hbm, box_of),
                (dev_hbm, dev),
                (off_hbm, off_of),
                (rate_hbm, rate_of),
                (cur_hbm, cur),
                (adj_hbm, adj),
                (rad_hbm, rad),
                (near_hbm, near),
                (inv_hbm, inv),
            ]
        )
    ]
    for copy in loads:
        copy.start()
    box_in, dev_in, off_in, rate_in, cur_in, adj_in, rad_in, near_in, inv_in = loads

    groups = [
        [(dx * nc + dc, at(dx=dx, dc=dc)) for dx in range(NX) for dc in range(nc) if dx or dc],
        [(dz, at(dz=dz)) for dz in range(1, NZ)],
        [(dy, at(dy=dy)) for dy in range(1, ny)],
    ]
    barrier = pltpu.get_barrier_semaphore()
    for group in groups:
        for _, device in group:
            pl.semaphore_signal(barrier, inc=1, device_id=device, device_id_type=MESH)

    for copy in (box_in, dev_in, off_in, rate_in):
        copy.wait()

    def column(values):
        return jnp.concatenate(
            [jnp.broadcast_to(values[:, k : k + 1], (blocks, 128)) for k in range(near_count)]
        )

    sub = lax.broadcasted_iota(jnp.int32, (pairs, 128), 0)
    lane = lax.broadcasted_iota(jnp.int32, (pairs, 128), 1)
    target = column(dev[...].astype(F32))
    target_row = jnp.sum(jnp.where(sub == lane, target, 0.0), axis=0, keepdims=True)
    rank = jnp.sum(
        jnp.where((target == target_row) & (sub < lane), 1.0, 0.0), axis=0, keepdims=True
    )
    device_row = target_row.astype(jnp.int32)
    far_x = (lax.shift_right_logical(device_row, 3) + (NX - x)) & (NX - 1)
    far_z = ((device_row & (NZ - 1)) + (NZ - z)) & (NZ - 1)
    place_row = jnp.zeros((1, 128), jnp.int32)
    for place, distance in enumerate(ORDER):
        place_row = jnp.where(far_z == distance, place, place_row)
    slot_row = ((far_x * NZ + place_row) * CAP).astype(F32) + rank
    slot_row = jnp.where(lane[0:1] < pairs, slot_row, -1.0)
    slot_col = jnp.sum(jnp.where(sub == lane, slot_row, 0.0), axis=1, keepdims=True)
    pair_id = ((sub & (blocks - 1)) * near_count + lax.shift_right_logical(sub, 3)).astype(F32)
    pair_row = jnp.sum(
        jnp.where(slot_col == lane.astype(F32), pair_id, 0.0), axis=0, keepdims=True
    )
    tab_v[...] = jnp.broadcast_to(pair_row, (8, 128)).astype(jnp.int32)
    tab_copy = pltpu.make_async_copy(tab_v, pair_tab, local_sem.at[9])
    tab_copy.start()

    slots = NX * NZ * CAP
    hot = jnp.where(
        slot_row == lax.broadcasted_iota(jnp.int32, (slots, 128), 0).astype(F32), 1.0, 0.0
    )
    rest = jnp.zeros((128 - pairs, 128), F32)
    off_col = jnp.concatenate([column(off_of[...].astype(F32)) + 1.0, rest])
    off_tab = (
        jnp.dot(hot.astype(BF16), off_col.astype(BF16), preferred_element_type=F32) - 1.0
    )
    row = lax.broadcasted_iota(jnp.int32, (blocks, 128), 0)
    box = jnp.zeros((blocks, 128), F32)
    for r in range(blocks):
        box = jnp.where(row == r, box_of[r].astype(F32), box)
    rate_box = jnp.where(
        lane < 64, column(rate_of[...]), jnp.concatenate([box] * near_count)
    )
    rate_box = jnp.dot(
        hot,
        jnp.concatenate([rate_box, rest]),
        precision=lax.Precision.HIGHEST,
        preferred_element_type=F32,
    )

    cur_in.wait()
    for r in range(blocks):
        re = pl.ds(2 * r, 16, stride=16)
        im = pl.ds(2 * r + 1, 16, stride=16)
        cur_at[PLACE[0], r, 0:2] = cur[re, :].reshape(2, 8, 128)
        cur_at[PLACE[0], r, 2:4] = cur[im, :].reshape(2, 8, 128)
    adj_in.wait()
    for r in range(blocks):
        re = pl.ds(2 * r, 16, stride=16)
        im = pl.ds(2 * r + 1, 16, stride=16)
        ar, ai = adj[re, :].astype(BF16), adj[im, :].astype(BF16)
        lhs[r, 0:16, 0:128] = ar
        lhs[r, 0:16, 128:256] = ai
        lhs[r, 16:32, 0:128] = ai
        lhs[r, 16:32, 128:256] = -ar
    rad_in.wait()
    far_re = jnp.zeros((16, 128), F32)
    far_im = jnp.zeros((16, 128), F32)
    for r in range(blocks):
        re = pl.ds(2 * r, 16, stride=16)
        im = pl.ds(2 * r + 1, 16, stride=16)
        rr, ri = rad[re, :], rad[im, :]
        cr, ci = cur[re, :], cur[im, :]
        far_re += rr * cr - ri * ci
        far_im += rr * ci + ri * cr
    far_tile = jnp.where(
        lane[0:16] < 64,
        jnp.sum(far_re, axis=1, keepdims=True),
        jnp.sum(far_im, axis=1, keepdims=True),
    )
    for k in range(NX):
        to = msg if k else msg_got
        rows = slice(k * NZ * CAP, (k + 1) * NZ * CAP)
        to[k, 0:16] = far_tile
        to[k, 16:40] = off_tab[rows]
        to[k, 40:64] = rate_box[rows]
    tab_copy.wait()
    near_in.wait()

    pl.semaphore_wait(barrier, sum(len(group) for group in groups))

    def halves(hops, way):
        return (0, 1) if hops < 4 else (way,)

    def cur_copy(way, step, h):
        sign = 1 if way == 0 else -1
        rows = slice(h * half, (h + 1) * half)
        return remote(
            cur_at.at[PLACE[(-sign * (step - 1)) % NZ], rows],
            cur_at.at[PLACE[(-sign * step) % NZ], rows],
            cur_s.at[way, step - 1, h],
            cur_r.at[way, step - 1, h],
            at(dz=sign % NZ),
        )

    cur_copies = {
        (way, step, h): cur_copy(way, step, h)
        for way in (0, 1)
        for step in range(1, 5)
        for h in halves(step, way)
    }

    def pass_currents(step, h):
        for way in (0, 1):
            cur_copies[way, step - 1, h].wait_recv()
            if h in halves(step, way):
                cur_copies[way, step, h].start()

    for h in (0, 1):
        for way in (0, 1):
            cur_copies[way, 1, h].start()

    def term_copy(place, k):
        return remote(
            sent.at[place, k - 1],
            got.at[place, k],
            term_s.at[place, k - 1],
            term_r.at[place, k - 1],
            at(dx=k),
        )

    def send_terms(place):
        for k in (2, 1, 3, 0):
            for s in range(CAP):
                pair = pair_tab[0, k * NZ * CAP + place * CAP + s]
                pair = jnp.clip(pair, 0, pairs - 1)
                term = jnp.dot(
                    lhs[lax.div(pair, near_count)], near[pair], preferred_element_type=F32
                ).reshape(4, 8, 128)
                if k:
                    sent[place, k - 1, s] = term
                else:
                    got[place, 0, s] = term
            if k:
                term_copy(place, k).start()

    def masks(place, k, s):
        at_row = 16 + place * CAP + s
        off = jnp.broadcast_to(msg_got[k, at_row : at_row + 1, :], (8, 128))
        return [(off == float(c))[None] for c in range(blocks)]

    def combine(place, to):
        for k in range(1, NX):
            term_copy(place, k).wait_recv()
        sums = [jnp.zeros((4, 8, 128), F32) for _ in range(blocks)]
        for k in range(NX):
            for s in range(CAP):
                term = got[place, k, s]
                for c, mask in enumerate(masks(place, k, s)):
                    sums[c] = sums[c] + jnp.where(mask, term, 0.0)
        for c in range(blocks):
            to(c)[...] = sums[c]

    def dots(place):
        for k in range(NX):
            for s in range(CAP):
                chosen = jnp.zeros((4, 8, 128), F32)
                for c, mask in enumerate(masks(place, k, s)):
                    chosen = jnp.where(mask, cur_at[place, c], chosen)
                product = jnp.sum(got[place, k, s] * chosen, axis=0)
                lane_dots[k, place * CAP + s : place * CAP + s + 1, :] = jnp.sum(
                    product, axis=0, keepdims=True
                )

    def part_copy(way, hops, h):
        rows = slice(h * half, (h + 1) * half)
        return remote(
            part.at[way, hops - 1, rows],
            part_got.at[way, hops - 1, rows],
            part_s.at[way, hops - 1, h],
            part_r.at[way, hops - 1, h],
            at(dz=1 if way == 0 else NZ - 1),
        )

    part_copies = {
        (way, hops, h): part_copy(way, hops, h)
        for way in (0, 1)
        for hops in range(1, 5)
        for h in halves(hops, way)
    }

    def combine_ring(hops):
        if hops == 4:
            combine(PLACE[4], lambda c: part.at[c // half, 3, c])
        else:
            combine(PLACE[hops], lambda c: part.at[0, hops - 1, c])
            combine(PLACE[NZ - hops], lambda c: part.at[1, hops - 1, c])

    def pass_sums(hops):
        for h in (0, 1):
            for way in (0, 1):
                if h in halves(hops + 1, way):
                    part_copies[way, hops + 1, h].wait_recv()
                    for c in range(h * half, (h + 1) * half):
                        part[way, hops - 1, c] += part_got[way, hops, c]
                part_copies[way, hops, h].start()

    msgs = [
        remote(msg.at[k], msg_got.at[k], msg_s.at[k], msg_r.at[k], at(dx=k))
        for k in range(1, NX)
    ]
    for copy in msgs:
        copy.start()
    send_terms(0)
    send_terms(1)
    pass_currents(2, 0)
    send_terms(2)
    pass_currents(2, 1)
    send_terms(3)
    for copy in msgs:
        copy.wait_recv()
    combine_ring(4)
    for way in (0, 1):
        part_copies[way, 4, way].start()
    pass_currents(3, 0)
    send_terms(4)
    pass_currents(3, 1)

    far_sum[...] = msg_got[0, 0:16] + msg_got[1, 0:16] + msg_got[2, 0:16] + msg_got[3, 0:16]
    fars = [
        remote(far_sum, far_got.at[k], far_s.at[k], far_r.at[k], at(dz=k)) for k in range(1, NZ)
    ]
    for copy in fars:
        copy.start()

    combine_ring(3)
    pass_sums(3)
    send_terms(5)
    pass_currents(4, 0)
    send_terms(6)
    pass_currents(4, 1)
    send_terms(7)
    combine_ring(2)
    pass_sums(2)
    combine_ring(1)
    for d in (1, 7, 2, 6, 3, 5):
        dots(PLACE[d])
    for way in (0, 1):
        cur_copies[way, 4, way].wait_recv()
    dots(PLACE[4])
    combine(PLACE[0], lambda c: own_sum.at[c])
    dots(PLACE[0])

    value = jnp.zeros((8, 128), F32)
    box_lane = lax.broadcasted_iota(jnp.int32, (NZ * CAP, 128), 1).astype(F32)
    for k in range(NX):
        rate = msg_got[k, 40:64, 0:1]
        box = msg_got[k, 40:64, 64:65]
        pair_value = rate * jnp.sum(lane_dots[k], axis=1, keepdims=True)
        table = jnp.where(box_lane == box, pair_value, 0.0)
        value += table[0:8] + table[8:16] + table[16:24]
    g_sum[0] = value

    g_all = [
        [
            remote(
                g_sum.at[stage],
                g_got.at[stage, place],
                g_s.at[stage, place],
                g_r.at[stage, place],
                device,
            )
            for place, device in groups[stage]
        ]
        for stage in range(3)
    ]

    def g_gather(stage):
        total = g_sum[stage]
        for (place, _), copy in zip(groups[stage], g_all[stage]):
            copy.wait_recv()
            total = total + g_got[stage, place]
        return total

    for copy in g_all[0]:
        copy.start()

    pass_sums(1)

    g_sum[1] = g_gather(0)
    for copy in g_all[1]:
        copy.start()

    for copy in fars:
        copy.wait_recv()
    far = far_sum[...]
    for k in range(1, NZ):
        far = far + far_got[k]
    far = far * norm_far
    far_re = jnp.broadcast_to(far[:, 0:1], (16, 128))
    far_im = jnp.broadcast_to(far[:, 64:65], (16, 128))

    def finish(h):
        for way in (0, 1):
            part_copies[way, 1, h].wait_recv()
        for c in range(h * half, (h + 1) * half):
            re = pl.ds(2 * c, 16, stride=16)
            im = pl.ds(2 * c + 1, 16, stride=16)
            rr, ri = rad[re, :], rad[im, :]
            total = (own_sum[c] + (part_got[0, 0, c] + part_got[1, 0, c])).reshape(32, 128)
            res_re = ((far_re * rr + far_im * ri) - total[0:16]).astype(BF16)
            res_im = ((far_im * rr - far_re * ri) - total[16:32]).astype(BF16)
            lhs[c, 0:16, 0:128] = res_re
            lhs[c, 0:16, 128:256] = res_im
            lhs[c, 16:32, 0:128] = res_im
            lhs[c, 16:32, 128:256] = -res_re
            update = jnp.dot(lhs[c], inv[c], preferred_element_type=F32)
            out[re, :] = adj[re, :] + update[0:16]
            out[im, :] = adj[im, :] + update[16:32]

    inv_in.wait()
    finish(0)
    g_sum[2] = g_gather(1)
    for copy in g_all[2]:
        copy.start()
    finish(1)
    total = jnp.sum(g_gather(2), axis=0, keepdims=True)
    grad[...] = jnp.broadcast_to(total, (8, 128))

    for copy in msgs + fars + g_all[0] + g_all[1] + g_all[2]:
        copy.wait_send()
    for copy in list(cur_copies.values()) + list(part_copies.values()):
        copy.wait_send()
    for place in range(NZ):
        for k in range(1, NX):
            term_copy(place, k).wait_send()


def on_device(
    adjoint,
    currents,
    radiation,
    near_blocks,
    inverse_blocks,
    col_device,
    col_offset,
    box_of_block,
    pair_rate,
):
    angles_here, blocks, unknowns = adjoint.shape[1], adjoint.shape[2], adjoint.shape[4]
    near_count = near_blocks.shape[1]
    pairs = blocks * near_count
    ny, nc = lax.axis_size("angle"), lax.axis_size("pol")
    basis_count = lax.axis_size("basis")
    rows = angles_here * blocks * 2

    vmem = pl.BlockSpec(memory_space=pltpu.VMEM)
    dma = pltpu.SemaphoreType.DMA
    sizes = (ny, nc, 1.0 / math.sqrt(blocks * basis_count * unknowns))
    out, grad = pl.pallas_call(
        functools.partial(kernel, sizes),
        out_shape=(
            jax.ShapeDtypeStruct((rows, unknowns), F32),
            jax.ShapeDtypeStruct((8, 128), F32),
        ),
        in_specs=[pl.BlockSpec(memory_space=pltpu.HBM)] * 9,
        out_specs=(vmem, vmem),
        scratch_shapes=[
            pltpu.SMEM((blocks,), jnp.int32),
            pltpu.VMEM((blocks, near_count), jnp.int32),
            pltpu.VMEM((blocks, near_count), jnp.int32),
            pltpu.VMEM((blocks, near_count), F32),
            pltpu.VMEM((rows, unknowns), F32),
            pltpu.VMEM((rows, unknowns), F32),
            pltpu.VMEM((rows, unknowns), F32),
            pltpu.VMEM((pairs, 2 * unknowns, unknowns), BF16),
            pltpu.VMEM((blocks, 2 * unknowns, unknowns), BF16),
            pltpu.VMEM((8, 128), jnp.int32),
            pltpu.SMEM((8, 128), jnp.int32),
            pltpu.VMEM((blocks, 32, 256), BF16),
            pltpu.VMEM((NZ, NX - 1, CAP, 4, 8, 128), F32),
            pltpu.VMEM((NZ, NX, CAP, 4, 8, 128), F32),
            pltpu.VMEM((NZ, blocks, 4, 8, 128), F32),
            pltpu.VMEM((2, 4, blocks, 4, 8, 128), F32),
            pltpu.VMEM((2, 4, blocks, 4, 8, 128), F32),
            pltpu.VMEM((blocks, 4, 8, 128), F32),
            pltpu.VMEM((NX, 64, 128), F32),
            pltpu.VMEM((NX, 64, 128), F32),
            pltpu.VMEM((16, 128), F32),
            pltpu.VMEM((NZ, 16, 128), F32),
            pltpu.VMEM((NX, NZ * CAP, 128), F32),
            pltpu.VMEM((3, 8, 128), F32),
            pltpu.VMEM((3, 8, 8, 128), F32),
            dma((10,)),
            dma((NZ, NX - 1)),
            dma((NZ, NX - 1)),
            dma((2, 4, 2)),
            dma((2, 4, 2)),
            dma((2, 4, 2)),
            dma((2, 4, 2)),
            dma((NX,)),
            dma((NX,)),
            dma((NZ,)),
            dma((NZ,)),
            dma((3, 8)),
            dma((3, 8)),
        ],
        compiler_params=pltpu.CompilerParams(
            collective_id=0, has_side_effects=True, vmem_limit_bytes=60 << 20
        ),
        name="sweep",
    )(
        box_of_block,
        col_device,
        col_offset,
        pair_rate,
        adjoint.reshape(rows, unknowns),
        currents.reshape(rows, unknowns),
        radiation.reshape(rows, unknowns),
        near_blocks.reshape(pairs, 2 * unknowns, unknowns),
        inverse_blocks.reshape(blocks, 2 * unknowns, unknowns),
    )
    me = lax.axis_index("basis")
    share = lax.dynamic_slice_in_dim(grad[0], me * BOX_DEV, BOX_DEV)
    angles_all = angles_here * ny
    shape_grad = share * (-1.0 / math.sqrt(4 * unknowns * angles_all * near_count))
    return (out.reshape(adjoint.shape), shape_grad)


def solution(mesh):
    placed = (
        P("pol", "angle", "basis", None, None),
        P("pol", "angle", "basis", None, None),
        P("pol", "angle", "basis", None, None),
        P("basis", None, None, None, None),
        P("basis", None, None, None),
        P("basis", None),
        P("basis", None),
        P("basis"),
        P("basis", None),
    )
    return jax.shard_map(
        on_device,
        mesh=mesh,
        in_specs=placed,
        out_specs=(P("pol", "angle", "basis", None, None), P("basis")),
        check_vma=False,
    )
```

time: 72.2 us -> 53.3 us (0.74)
  Pallas kernels: 60.3 us -> 49.6 us
  local copies, waits for them, and re-layouts: 9.05 us -> 2.25 us
  other arithmetic: 1.8 us -> 0.58 us
    pallas_call x1, Pallas kernels: 60.3 us -> 49.6 us  [on_device(): pl.pallas_call(functools.partial(kernel, sizes), out_shape=(jax.ShapeDtyp...]
    unnamed x11 -> x1, local copies, waits for them, and re-layouts: 6.3 us -> 1.57 us
    broadcast_in_dim x5 -> x0, local copies, waits for them, and re-layouts: 1.73 us -> none  [the longest x1 0.77 us: on_device(): rate = jnp.sum(jnp.where(hot, pair_rate.reshape(1, pairs), 0.0), axis=1)]
    reshape x1 -> x0, local copies, waits for them, and re-layouts: 0.77 us -> none  [on_device(): target = col_device.reshape(pairs)]
    add x2 -> x0, other arithmetic: 0.72 us -> none  [the longest x1 0.69 us: on_device(): col_offset.reshape(1, pairs) + 1]
where the time goes in v2:
time: 53.3 us; the launch traced here: 53.1 us
  Pallas kernels  49.6 us (93%)
  local copies, waits for them, and re-layouts  2.25 us (4%)
  between operations  0.65 us (1%)
  other arithmetic  0.58 us (1%)
    pallas_call x1, Pallas kernels, on_device(): pl.pallas_call(functools.partial(kernel, sizes), out_shape=(jax.ShapeDtyp...  49.6 us
    unnamed x1, local copies, waits for them, and re-layouts  1.57 us

profile of v2, /device:TPU:1, one launch (start us, length us, event | category | flops | bytes accessed | tf_op | source)
XLA Modules:
  0.0 53.1 jit_solution(17698752277606881792)
XLA Ops:
  0.6 49.6 %sweep.1 = (f32[256,128]{1,0:T(8,128)}, f32[8,128]{1,0:T(8,128)}) custom-call(s32[8]{0:T(128)} %box_hbm.1, s32[8,6]{1,0:T(8,128)} %dev_hbm.1, s32[8,6]{1,0:T(8,128)} %off_hbm.1, f32[8,6]{1,0:T(8,128)} %rate_hbm.1, f32[256,128]{1,0:T(8,128)} %bitcast.10, f32[256,128]{1,0:T(8,128)} %bitcast.11, f32[256,128]{1,0:T(8,128)} %bitcast.12, ...), custom_call_target="tpu_custom_call" | custom-call | tf_op jit(solution)/shard_map/sweep/pallas_call | solution.py:492
  50.3 0.7 %slice.3 = f32[1,128]{1,0:T(1,128)S(1)} slice(f32[8,128]{1,0:T(8,128)} %get-tuple-element.5), slice={[0:1], [0:128]} | slice | bytes 1024 | tf_op jit(solution)/shard_map/slice | solution.py:556
  50.9 0.6 %multiply_bitcast_fusion = f32[4]{0:T(128)} fusion(f32[1,128]{1,0:T(1,128)S(1)} %slice.3, s32[]{:T(128)S(6)} %select_n.3), kind=kLoop, calls=%fused_computation | loop fusion | flops 4 | bytes 36 | tf_op jit(solution)/shard_map/mul | solution.py:558
  51.5 1.6 %copy.12 = f32[1,16,8,2,128]{4,3,2,1,0:T(2,128)} copy(f32[1,16,8,2,128]{4,3,2,1,0:T(2,128)} %bitcast.13) | data formatting | bytes 262144

commit v3 on v2

--- a/solution.py
+++ b/solution.py
@@ -71,7 +71,7 @@
     g_s,
     g_r,
 ):
-    ny, nc, norm_far = sizes
+    ny, nc, norm_far, grad_norm = sizes
     blocks, near_count = 8, 6
     pairs = blocks * near_count
     half = blocks // 2
@@ -276,6 +276,10 @@
             if k:
                 term_copy(place, k).start()
 
+    def terms_gone(place):
+        for k in range(1, NX):
+            term_copy(place, k).wait_send()
+
     def masks(place, k, s):
         at_row = 16 + place * CAP + s
         off = jnp.broadcast_to(msg_got[k, at_row : at_row + 1, :], (8, 128))
@@ -357,14 +361,12 @@
     pass_currents(3, 0)
     send_terms(4)
     pass_currents(3, 1)
-
     far_sum[...] = msg_got[0, 0:16] + msg_got[1, 0:16] + msg_got[2, 0:16] + msg_got[3, 0:16]
     fars = [
         remote(far_sum, far_got.at[k], far_s.at[k], far_r.at[k], at(dz=k)) for k in range(1, NZ)
     ]
     for copy in fars:
         copy.start()
-
     combine_ring(3)
     pass_sums(3)
     send_terms(5)
@@ -375,8 +377,12 @@
     combine_ring(2)
     pass_sums(2)
     combine_ring(1)
-    for d in (1, 7, 2, 6, 3, 5):
-        dots(PLACE[d])
+    dots(PLACE[1])
+    dots(PLACE[7])
+    dots(PLACE[2])
+    dots(PLACE[6])
+    dots(PLACE[3])
+    dots(PLACE[5])
     for way in (0, 1):
         cur_copies[way, 4, way].wait_recv()
     dots(PLACE[4])
@@ -416,9 +422,7 @@
 
     for copy in g_all[0]:
         copy.start()
-
     pass_sums(1)
-
     g_sum[1] = g_gather(0)
     for copy in g_all[1]:
         copy.start()
@@ -457,15 +461,16 @@
         copy.start()
     finish(1)
     total = jnp.sum(g_gather(2), axis=0, keepdims=True)
-    grad[...] = jnp.broadcast_to(total, (8, 128))
+    for i in range(BOX_DEV):
+        mine = lane[0:1] == b * BOX_DEV + i
+        grad[:, i : i + 1] = jnp.sum(jnp.where(mine, total, 0.0), axis=1, keepdims=True) * grad_norm
 
     for copy in msgs + fars + g_all[0] + g_all[1] + g_all[2]:
         copy.wait_send()
     for copy in list(cur_copies.values()) + list(part_copies.values()):
         copy.wait_send()
-    for place in range(NZ):
-        for k in range(1, NX):
-            term_copy(place, k).wait_send()
+    for place in (0, 1, 2, 3, 4, 5, 6, 7):
+        terms_gone(place)
 
 
 def on_device(
@@ -488,12 +493,17 @@
 
     vmem = pl.BlockSpec(memory_space=pltpu.VMEM)
     dma = pltpu.SemaphoreType.DMA
-    sizes = (ny, nc, 1.0 / math.sqrt(blocks * basis_count * unknowns))
+    sizes = (
+        ny,
+        nc,
+        1.0 / math.sqrt(blocks * basis_count * unknowns),
+        -1.0 / math.sqrt(4 * unknowns * angles_here * ny * near_count),
+    )
     out, grad = pl.pallas_call(
         functools.partial(kernel, sizes),
         out_shape=(
             jax.ShapeDtypeStruct((rows, unknowns), F32),
-            jax.ShapeDtypeStruct((8, 128), F32),
+            jax.ShapeDtypeStruct((1, BOX_DEV), F32),
         ),
         in_specs=[pl.BlockSpec(memory_space=pltpu.HBM)] * 9,
         out_specs=(vmem, vmem),
@@ -538,10 +548,10 @@
             dma((3, 8)),
         ],
         compiler_params=pltpu.CompilerParams(
-            collective_id=0, has_side_effects=True, vmem_limit_bytes=60 << 20
+            collective_id=0, has_side_effects=True, vmem_limit_bytes=40 << 20
         ),
         name="sweep",
-    )(
+    )(*[pltpu.with_memory_space_constraint(a, pltpu.HBM) for a in (
         box_of_block,
         col_device,
         col_offset,
@@ -551,12 +561,8 @@
         radiation.reshape(rows, unknowns),
         near_blocks.reshape(pairs, 2 * unknowns, unknowns),
         inverse_blocks.reshape(blocks, 2 * unknowns, unknowns),
-    )
-    me = lax.axis_index("basis")
-    share = lax.dynamic_slice_in_dim(grad[0], me * BOX_DEV, BOX_DEV)
-    angles_all = angles_here * ny
-    shape_grad = share * (-1.0 / math.sqrt(4 * unknowns * angles_all * near_count))
-    return (out.reshape(adjoint.shape), shape_grad)
+    )])
+    return (out.reshape(adjoint.shape), grad.reshape(BOX_DEV))
 
 
 def solution(mesh):

time: 53.3 us -> 51 us (0.957)
  local copies, waits for them, and re-layouts: 2.25 us -> 1.17 us
  Pallas kernels: 49.6 us -> 49 us
  other arithmetic: 0.58 us -> 0 us
    slice x1 -> x0, local copies, waits for them, and re-layouts: 0.69 us -> none  [on_device(): share = lax.dynamic_slice_in_dim(grad[0], me * BOX_DEV, BOX_DEV)]
    mul x1 -> x0, other arithmetic: 0.58 us -> none  [on_device(): share * (-1.0 / math.sqrt(4 * unknowns * angles_all * near_count))]
    pallas_call x1, Pallas kernels: 49.6 us -> 49 us  [on_device(): pl.pallas_call(functools.partial(kernel, sizes), out_shape=(jax.ShapeDtyp...]
    unnamed x1 -> x2, local copies, waits for them, and re-layouts: 1.57 us -> 1.17 us
where the time goes in v3:
time: 51 us; the launch traced here: 50.8 us
  Pallas kernels  49 us (96%)
  local copies, waits for them, and re-layouts  1.17 us (2%)
  between operations  0.64 us (1%)
    pallas_call x1, Pallas kernels, on_device(): pl.pallas_call(functools.partial(kernel, sizes), out_shape=(jax.ShapeDtyp...  49 us
    unnamed x2, local copies, waits for them, and re-layouts  1.17 us

profile of v3, /device:TPU:1, one launch (start us, length us, event | category | flops | bytes accessed | tf_op | source)
XLA Modules:
  0.0 50.8 jit_solution(17038814964926331812)
XLA Ops:
  0.6 49.0 %sweep.1 = (f32[256,128]{1,0:T(8,128)S(1)}, f32[1,4]{1,0:T(1,128)S(1)}) custom-call(s32[8]{0:T(128)} %box_hbm.1, s32[8,6]{1,0:T(8,128)} %dev_hbm.1, s32[8,6]{1,0:T(8,128)} %off_hbm.1, f32[8,6]{1,0:T(8,128)} %rate_hbm.1, f32[256,128]{1,0:T(8,128)} %bitcast.11, f32[256,128]{1,0:T(8,128)} %bitcast.12, f32[256,128]{1,0:T(8,128)} %bitcast.13, ...), custom_call_target="tpu_custom_call" | custom-call | tf_op jit(solution)/shard_map/sweep/pallas_call | solution.py:502
  49.7 0.7 %copy.13 = f32[1,16,8,2,128]{4,3,2,1,0:T(2,128)} copy(f32[1,16,8,2,128]{4,3,2,1,0:T(2,128)S(1)} %bitcast.7) | data formatting | bytes 262144
  50.3 0.5 %copy.14 = f32[4]{0:T(128)} copy(f32[4]{0:T(128)S(1)} %bitcast.8) | data formatting | bytes 32

commit v4 on v3

--- a/solution.py
+++ b/solution.py
@@ -397,7 +397,7 @@
         pair_value = rate * jnp.sum(lane_dots[k], axis=1, keepdims=True)
         table = jnp.where(box_lane == box, pair_value, 0.0)
         value += table[0:8] + table[8:16] + table[16:24]
-    g_sum[0] = value
+    g_sum[0] = jnp.sum(value, axis=0, keepdims=True)
 
     g_all = [
         [
@@ -460,17 +460,19 @@
     for copy in g_all[2]:
         copy.start()
     finish(1)
-    total = jnp.sum(g_gather(2), axis=0, keepdims=True)
-    for i in range(BOX_DEV):
-        mine = lane[0:1] == b * BOX_DEV + i
-        grad[:, i : i + 1] = jnp.sum(jnp.where(mine, total, 0.0), axis=1, keepdims=True) * grad_norm
-
-    for copy in msgs + fars + g_all[0] + g_all[1] + g_all[2]:
+    for copy in msgs + fars + g_all[0] + g_all[1]:
         copy.wait_send()
     for copy in list(cur_copies.values()) + list(part_copies.values()):
         copy.wait_send()
     for place in (0, 1, 2, 3, 4, 5, 6, 7):
         terms_gone(place)
+    total = g_gather(2)
+    for i in range(BOX_DEV):
+        mine = lane[0:1] == b * BOX_DEV + i
+        grad[:, i : i + 1] = jnp.sum(jnp.where(mine, total, 0.0), axis=1, keepdims=True) * grad_norm
+
+    for copy in g_all[2]:
+        copy.wait_send()
 
 
 def on_device(
@@ -531,8 +533,8 @@
             pltpu.VMEM((16, 128), F32),
             pltpu.VMEM((NZ, 16, 128), F32),
             pltpu.VMEM((NX, NZ * CAP, 128), F32),
-            pltpu.VMEM((3, 8, 128), F32),
-            pltpu.VMEM((3, 8, 8, 128), F32),
+            pltpu.VMEM((3, 1, 128), F32),
+            pltpu.VMEM((3, 8, 1, 128), F32),
             dma((10,)),
             dma((NZ, NX - 1)),
             dma((NZ, NX - 1)),

time: 51 us -> 50 us (0.980)
  Pallas kernels: 49 us -> 48.1 us
    pallas_call x1, Pallas kernels: 49 us -> 48.1 us  [on_device(): pl.pallas_call(functools.partial(kernel, sizes), out_shape=(jax.ShapeDtyp...]
where the time goes in v4:
time: 50 us; the launch traced here: 49.9 us
  Pallas kernels  48.1 us (96%)
  local copies, waits for them, and re-layouts  1.17 us (2%)
  between operations  0.64 us (1%)
    pallas_call x1, Pallas kernels, on_device(): pl.pallas_call(functools.partial(kernel, sizes), out_shape=(jax.ShapeDtyp...  48.1 us
    unnamed x2, local copies, waits for them, and re-layouts  1.17 us

profile of v4, /device:TPU:1, one launch (start us, length us, event | category | flops | bytes accessed | tf_op | source)
XLA Modules:
  0.0 49.9 jit_solution(13039450506250449806)
XLA Ops:
  0.6 48.1 %sweep.1 = (f32[256,128]{1,0:T(8,128)S(1)}, f32[1,4]{1,0:T(1,128)S(1)}) custom-call(s32[8]{0:T(128)} %box_hbm.1, s32[8,6]{1,0:T(8,128)} %dev_hbm.1, s32[8,6]{1,0:T(8,128)} %off_hbm.1, f32[8,6]{1,0:T(8,128)} %rate_hbm.1, f32[256,128]{1,0:T(8,128)} %bitcast.11, f32[256,128]{1,0:T(8,128)} %bitcast.12, f32[256,128]{1,0:T(8,128)} %bitcast.13, ...), custom_call_target="tpu_custom_call" | custom-call | tf_op jit(solution)/shard_map/sweep/pallas_call | solution.py:504
  48.7 0.7 %copy.13 = f32[1,16,8,2,128]{4,3,2,1,0:T(2,128)} copy(f32[1,16,8,2,128]{4,3,2,1,0:T(2,128)S(1)} %bitcast.7) | data formatting | bytes 262144
  49.4 0.5 %copy.14 = f32[4]{0:T(128)} copy(f32[4]{0:T(128)S(1)} %bitcast.8) | data formatting | bytes 32

commit v5 on v4

--- a/solution.py
+++ b/solution.py
@@ -285,9 +285,12 @@
         off = jnp.broadcast_to(msg_got[k, at_row : at_row + 1, :], (8, 128))
         return [(off == float(c))[None] for c in range(blocks)]
 
+    def arrive(*places):
+        for place in places:
+            for k in range(1, NX):
+                term_copy(place, k).wait_recv()
+
     def combine(place, to):
-        for k in range(1, NX):
-            term_copy(place, k).wait_recv()
         sums = [jnp.zeros((4, 8, 128), F32) for _ in range(blocks)]
         for k in range(NX):
             for s in range(CAP):
@@ -355,6 +358,7 @@
     send_terms(3)
     for copy in msgs:
         copy.wait_recv()
+    arrive(PLACE[4])
     combine_ring(4)
     for way in (0, 1):
         part_copies[way, 4, way].start()
@@ -367,6 +371,7 @@
     ]
     for copy in fars:
         copy.start()
+    arrive(PLACE[3], PLACE[5])
     combine_ring(3)
     pass_sums(3)
     send_terms(5)
@@ -374,9 +379,10 @@
     send_terms(6)
     pass_currents(4, 1)
     send_terms(7)
+    arrive(PLACE[2], PLACE[6])
     combine_ring(2)
     pass_sums(2)
-    combine_ring(1)
+    arrive(PLACE[1], PLACE[7])
     dots(PLACE[1])
     dots(PLACE[7])
     dots(PLACE[2])
@@ -386,7 +392,7 @@
     for way in (0, 1):
         cur_copies[way, 4, way].wait_recv()
     dots(PLACE[4])
-    combine(PLACE[0], lambda c: own_sum.at[c])
+    arrive(PLACE[0])
     dots(PLACE[0])
 
     value = jnp.zeros((8, 128), F32)
@@ -422,7 +428,9 @@
 
     for copy in g_all[0]:
         copy.start()
+    combine_ring(1)
     pass_sums(1)
+    combine(PLACE[0], lambda c: own_sum.at[c])
     g_sum[1] = g_gather(0)
     for copy in g_all[1]:
         copy.start()

time: 50 us -> 50 us (level)
  no operation moved by 1% of the time
where the time goes in v5:
time: 50 us; the launch traced here: 49.9 us
  Pallas kernels  48.1 us (96%)
  local copies, waits for them, and re-layouts  1.17 us (2%)
  between operations  0.64 us (1%)
    pallas_call x1, Pallas kernels, on_device(): pl.pallas_call(functools.partial(kernel, sizes), out_shape=(jax.ShapeDtyp...  48.1 us
    unnamed x2, local copies, waits for them, and re-layouts  1.17 us

profile of v5, /device:TPU:1, one launch (start us, length us, event | category | flops | bytes accessed | tf_op | source)
XLA Modules:
  0.0 49.9 jit_solution(10220097812413637755)
XLA Ops:
  0.6 48.1 %sweep.1 = (f32[256,128]{1,0:T(8,128)S(1)}, f32[1,4]{1,0:T(1,128)S(1)}) custom-call(s32[8]{0:T(128)} %box_hbm.1, s32[8,6]{1,0:T(8,128)} %dev_hbm.1, s32[8,6]{1,0:T(8,128)} %off_hbm.1, f32[8,6]{1,0:T(8,128)} %rate_hbm.1, f32[256,128]{1,0:T(8,128)} %bitcast.11, f32[256,128]{1,0:T(8,128)} %bitcast.12, f32[256,128]{1,0:T(8,128)} %bitcast.13, ...), custom_call_target="tpu_custom_call" | custom-call | tf_op jit(solution)/shard_map/sweep/pallas_call | solution.py:512
  48.7 0.7 %copy.13 = f32[1,16,8,2,128]{4,3,2,1,0:T(2,128)} copy(f32[1,16,8,2,128]{4,3,2,1,0:T(2,128)S(1)} %bitcast.7) | data formatting | bytes 262144
  49.4 0.5 %copy.14 = f32[4]{0:T(128)} copy(f32[4]{0:T(128)S(1)} %bitcast.8) | data formatting | bytes 32

commit v6 on v5

--- a/solution.py
+++ b/solution.py
@@ -380,8 +380,6 @@
     pass_currents(4, 1)
     send_terms(7)
     arrive(PLACE[2], PLACE[6])
-    combine_ring(2)
-    pass_sums(2)
     arrive(PLACE[1], PLACE[7])
     dots(PLACE[1])
     dots(PLACE[7])
@@ -428,6 +426,8 @@
 
     for copy in g_all[0]:
         copy.start()
+    combine_ring(2)
+    pass_sums(2)
     combine_ring(1)
     pass_sums(1)
     combine(PLACE[0], lambda c: own_sum.at[c])

time: 50 us -> 54.5 us (1.090)
  the two profiles are of different devices: /device:TPU:1 before, /device:TPU:8 now
where the time goes in v6:
time: 54.5 us; the launch traced here: 54.3 us
  Pallas kernels  52.5 us (96%)
  local copies, waits for them, and re-layouts  1.17 us (2%)
  between operations  0.64 us (1%)
    pallas_call x1, Pallas kernels, on_device(): pl.pallas_call(functools.partial(kernel, sizes), out_shape=(jax.ShapeDtyp...  52.5 us
    unnamed x2, local copies, waits for them, and re-layouts  1.17 us

profile of v6, /device:TPU:8, one launch (start us, length us, event | category | flops | bytes accessed | tf_op | source)
XLA Modules:
  0.0 54.3 jit_solution(8326161594785285039)
XLA Ops:
  0.6 52.5 %sweep.1 = (f32[256,128]{1,0:T(8,128)S(1)}, f32[1,4]{1,0:T(1,128)S(1)}) custom-call(s32[8]{0:T(128)} %box_hbm.1, s32[8,6]{1,0:T(8,128)} %dev_hbm.1, s32[8,6]{1,0:T(8,128)} %off_hbm.1, f32[8,6]{1,0:T(8,128)} %rate_hbm.1, f32[256,128]{1,0:T(8,128)} %bitcast.11, f32[256,128]{1,0:T(8,128)} %bitcast.12, f32[256,128]{1,0:T(8,128)} %bitcast.13, ...), custom_call_target="tpu_custom_call" | custom-call | tf_op jit(solution)/shard_map/sweep/pallas_call | solution.py:512
  53.2 0.7 %copy.13 = f32[1,16,8,2,128]{4,3,2,1,0:T(2,128)} copy(f32[1,16,8,2,128]{4,3,2,1,0:T(2,128)S(1)} %bitcast.7) | data formatting | bytes 262144
  53.8 0.5 copy.14
